TPU v7x, 32 devices: a whole 2x2x4 slice. The times are simulated.
32 devices in a mesh: gs: 8 (over z, y), img: 4 (over x, core).
Axes of the slice: x: 2, y: 2, z: 4, core: 2. Of those that a mesh axis runs over, the one named last changes fastest.
Arguments:
- gaussians: float32 [59, 40960], P(None, ('gs', 'img')), may hold values from -6 to 2048, as said below
- send_slots: int32 [32, 2560], P(('gs', 'img')), may hold values from 0 to 1279, as said below
- tile_lists: int32 [32, 128, 512], P('img', 'gs'), may hold values from -1 to 2559, as said below
- truth: float32 [3, 512, 2048], P(None, 'img', 'gs'), may hold values from 0 to 1
Outputs:
- rendered: float32 [3, 512, 2048], P(None, 'img', 'gs')
- pixel_loss: float32 [512, 2048], P('img', 'gs')
Inputs may be any that keep to these rules, and one draw needn't show every extreme that they name: `gaussians`: rows 0 and 1 are pixel positions, row 2 a depth of 10 to 60, rows 3 to 5 log scales, rows 6 to 9 a quaternion whose first component is at least 0.5, row 10 an opacity logit, rows 11 to 58 colour harmonics, 16 for each channel. `send_slots`: row s lists, for each destination device in order, 80 indices of source s's own Gaussians. `tile_lists`: live entries (0 or more) name distinct slots of the owning device's received Gaussians and come first, ordered by increasing depth (row 2) of the Gaussians they name; the rest are -1.
All inputs are finite; a program needn't handle non-finite values.
Results may differ from a plain program's by a relative error of at most 0.0003.
Values sent between devices are 32-bit elements; how exact they have to be, the bound alone decides.
No kernel may reach another device: no remote copies, remote signals or barrier semaphores. Data moves between devices by JAX's collectives and lax.ppermute only.
A program may use at most 64 MiB of HBM per device.

v0:
```python
import jax
import jax.numpy as jnp
from jax import lax
from jax.sharding import PartitionSpec as P

TILE = 16


coef_zero = 0.28209479177387814
coef_one = 0.4886025119029199
coef_two = [
    1.0925484305920792,
    -1.0925484305920792,
    0.31539156525252005,
    -1.0925484305920792,
    0.5462742152960396,
]
coef_three = [
    -0.5900435899266435,
    2.890611442640554,
    -0.4570457994644658,
    0.3731763325901154,
    -0.4570457994644658,
    1.445305721320277,
    -0.5900435899266435,
]
camera_z = -3000.0
ssim_share = 0.2
stable_one = 0.0001
stable_two = 0.0009


def extended(value, sides, width):
    for axis, dim in sides:
        size, length = (lax.axis_size(axis), value.shape[dim])
        up = [(i, (i + 1) % size) for i in range(size - 1)]
        down = [(j, i) for i, j in up]
        last = lax.slice_in_dim(value, length - width, length, axis=dim)
        first = lax.slice_in_dim(value, 0, width, axis=dim)
        before = lax.ppermute(last, axis, up)
        after = lax.ppermute(first, axis, down)
        value = jnp.concatenate([before, value, after], axis=dim)
    return value


def project(gauss):
    mean_x, mean_y, mean_z = (gauss[0], gauss[1], gauss[2])
    squared = jnp.exp(2.0 * gauss[3:6])
    rotation = gauss[6:10] / jnp.sqrt(jnp.sum(gauss[6:10] * gauss[6:10], axis=0))
    quat_w, quat_x, quat_y, quat_z = (rotation[0], rotation[1], rotation[2], rotation[3])
    first_a = 1.0 - 2.0 * (quat_y * quat_y + quat_z * quat_z)
    first_b = 2.0 * (quat_x * quat_y - quat_w * quat_z)
    first_c = 2.0 * (quat_x * quat_z + quat_w * quat_y)
    second_a = 2.0 * (quat_x * quat_y + quat_w * quat_z)
    second_b = 1.0 - 2.0 * (quat_x * quat_x + quat_z * quat_z)
    second_c = 2.0 * (quat_y * quat_z - quat_w * quat_x)
    cov_xx = (
        first_a * first_a * squared[0]
        + first_b * first_b * squared[1]
        + first_c * first_c * squared[2]
        + 0.3
    )
    cov_xy = (
        first_a * second_a * squared[0]
        + first_b * second_b * squared[1]
        + first_c * second_c * squared[2]
    )
    cov_yy = (
        second_a * second_a * squared[0]
        + second_b * second_b * squared[1]
        + second_c * second_c * squared[2]
        + 0.3
    )
    determinant = cov_xx * cov_yy - cov_xy * cov_xy
    opacity = jax.nn.sigmoid(gauss[10])
    delta_z = mean_z - camera_z
    length = jnp.sqrt(mean_x * mean_x + mean_y * mean_y + delta_z * delta_z)
    dir_x, dir_y, dir_z = (mean_x / length, mean_y / length, delta_z / length)
    sq_x, sq_y, sq_z = (dir_x * dir_x, dir_y * dir_y, dir_z * dir_z)
    prod_xy, prod_yz, prod_xz = (dir_x * dir_y, dir_y * dir_z, dir_x * dir_z)
    harmonic_basis = jnp.stack(
        [
            coef_zero * jnp.ones_like(dir_x),
            -coef_one * dir_y,
            coef_one * dir_z,
            -coef_one * dir_x,
            coef_two[0] * prod_xy,
            coef_two[1] * prod_yz,
            coef_two[2] * (2.0 * sq_z - sq_x - sq_y),
            coef_two[3] * prod_xz,
            coef_two[4] * (sq_x - sq_y),
            coef_three[0] * dir_y * (3.0 * sq_x - sq_y),
            coef_three[1] * prod_xy * dir_z,
            coef_three[2] * dir_y * (4.0 * sq_z - sq_x - sq_y),
            coef_three[3] * dir_z * (2.0 * sq_z - 3.0 * sq_x - 3.0 * sq_y),
            coef_three[4] * dir_x * (4.0 * sq_z - sq_x - sq_y),
            coef_three[5] * dir_z * (sq_x - sq_y),
            coef_three[6] * dir_x * (sq_x - 3.0 * sq_y),
        ]
    )
    harmonics = gauss[11:59].reshape(3, 16, gauss.shape[1])
    colour = jnp.maximum(jnp.sum(harmonics * harmonic_basis[None], axis=1) + 0.5, 0.0)
    return jnp.stack(
        [
            mean_x,
            mean_y,
            cov_yy / determinant,
            -cov_xy / determinant,
            cov_xx / determinant,
            opacity,
            colour[0],
            colour[1],
            colour[2],
        ]
    )


def splat_alpha(params, live_mask, pix_x, pix_y):
    delta_x = pix_x[:, :, None] - params[0][:, None, :]
    delta_y = pix_y[:, :, None] - params[1][:, None, :]
    power = -0.5 * (
        params[2][:, None, :] * delta_x * delta_x + params[4][:, None, :] * delta_y * delta_y
    )
    power = power - params[3][:, None, :] * delta_x * delta_y
    return jnp.where(live_mask[:, None, :], params[5][:, None, :] * jnp.exp(power), 0.0)


def window():
    offsets = jnp.arange(11, dtype=jnp.float32) - 5.0
    weights = jnp.exp(-offsets * offsets / 4.5)
    return weights / jnp.sum(weights)


def band_matrix(outputs, inputs_len, sign):
    difference = sign * (
        jnp.arange(inputs_len, dtype=jnp.int32)[None, :]
        - jnp.arange(outputs, dtype=jnp.int32)[:, None]
    )
    offsets = jnp.arange(11, dtype=jnp.int32)
    return jnp.sum(
        jnp.where(difference[:, :, None] == offsets[None, None, :], window()[None, None, :], 0.0),
        axis=2,
    )


def loss_from(filtered, rendered, truth):
    mean_r, mean_t = (filtered[0:3], filtered[3:6])
    variance_r = filtered[6:9] - mean_r * mean_r
    variance_t = filtered[9:12] - mean_t * mean_t
    covariance = filtered[12:15] - mean_r * mean_t
    similarity = (
        (2.0 * mean_r * mean_t + stable_one)
        * (2.0 * covariance + stable_two)
        / (
            (mean_r * mean_r + mean_t * mean_t + stable_one)
            * (variance_r + variance_t + stable_two)
        )
    )
    return (1.0 - ssim_share) * jnp.mean(jnp.abs(rendered - truth), axis=0) + ssim_share * (
        1.0 - jnp.mean(similarity, axis=0)
    )


def on_device(gaussians, send_slots, tile_lists, truth):
    local_index = send_slots[0]
    outgoing = gaussians[:, local_index]
    arrived = lax.all_to_all(outgoing, ("gs", "img"), split_axis=1, concat_axis=1, tiled=True)
    splats = project(arrived)
    rows_here, cols_here, list_len = tile_lists.shape
    tile_count = rows_here * cols_here
    group_size = 32
    groups = tile_count // group_size
    flat_lists = tile_lists.reshape(tile_count, list_len)
    tile_number = jnp.arange(tile_count, dtype=jnp.int32)
    tile_row = lax.axis_index("img") * rows_here + tile_number // cols_here
    tile_col = lax.axis_index("gs") * cols_here + tile_number % cols_here
    pixels = jnp.arange(TILE * TILE, dtype=jnp.int32)
    pix_x = (tile_col[:, None] * TILE + pixels[None, :] % TILE).astype(jnp.float32) + 0.5
    pix_y = (tile_row[:, None] * TILE + pixels[None, :] // TILE).astype(jnp.float32) + 0.5
    live_blocks = (jnp.sum((flat_lists >= 0).astype(jnp.int32), axis=1) + 127) // 128
    group_blocks = jnp.max(live_blocks.reshape(groups, group_size), axis=1)
    strict = (jnp.arange(128)[:, None] < jnp.arange(128)[None, :]).astype(jnp.float32)

    def render_group(inputs):
        group_lists, group_x, group_y, block_limit = inputs

        def blend_block(block_index, state_pair):
            log_left, colour = state_pair
            block_lists = lax.dynamic_slice_in_dim(group_lists, block_index * 128, 128, 1)
            block_live = block_lists >= 0
            block_params = splats[:, jnp.maximum(block_lists, 0)]
            alphas = splat_alpha(block_params, block_live, group_x, group_y)
            log_keep = jnp.log1p(-alphas)
            before = jnp.einsum("tpk,kj->tpj", log_keep, strict, precision=lax.Precision.HIGHEST)
            weight = jnp.exp(log_left[:, :, None] + before) * alphas
            colour = colour + jnp.einsum(
                "tpk,ctk->ctp", weight, block_params[6:9], precision=lax.Precision.HIGHEST
            )
            return (log_left + jnp.sum(log_keep, axis=2), colour)

        initial = (
            jnp.zeros((group_size, TILE * TILE), jnp.float32),
            jnp.zeros((3, group_size, TILE * TILE), jnp.float32),
        )
        return lax.fori_loop(0, block_limit, blend_block, initial)[1]

    colours = lax.map(
        render_group,
        (
            flat_lists.reshape(groups, group_size, list_len),
            pix_x.reshape(groups, group_size, TILE * TILE),
            pix_y.reshape(groups, group_size, TILE * TILE),
            group_blocks,
        ),
    )
    rendered = (
        colours.transpose(1, 0, 2, 3)
        .reshape(3, rows_here, cols_here, TILE, TILE)
        .transpose(0, 1, 3, 2, 4)
    )
    rendered = rendered.reshape(3, rows_here * TILE, cols_here * TILE)
    stacked = jnp.concatenate([rendered, truth])
    padded = extended(stacked, (("gs", 2), ("img", 1)), 5)
    rim_r, rim_t = (padded[0:3], padded[3:6])
    quantities = jnp.concatenate([rim_r, rim_t, rim_r * rim_r, rim_t * rim_t, rim_r * rim_t])
    img_height, img_width = (rendered.shape[1], rendered.shape[2])
    band_rows = band_matrix(img_height, img_height + 10, 1)
    band_cols = band_matrix(img_width, img_width + 10, 1).T
    filtered = jnp.einsum("ij,cjw->ciw", band_rows, quantities, precision=lax.Precision.HIGHEST)
    filtered = jnp.einsum("ciw,wv->civ", filtered, band_cols, precision=lax.Precision.HIGHEST)
    return (rendered, loss_from(filtered, rendered, truth))


def solution(mesh):
    return jax.shard_map(
        on_device,
        mesh=mesh,
        in_specs=(
            P(None, ("gs", "img")),
            P(("gs", "img"), None),
            P("img", "gs", None),
            P(None, "img", "gs"),
        ),
        out_specs=(P(None, "img", "gs"), P("img", "gs")),
        check_vma=False,
    )
```

profile of v0, /device:TPU:0, one launch (start us, length us, event | category | flops | bytes accessed | tf_op | source)
XLA Modules:
  0.0 678.7 jit_solution(16791380547998474627)
XLA Ops:
  20.9 20.9 %all-to-all-done = f32[59,32,80]{2,0,1:T(8,128)S(1)} async-done(((f32[59,32,80]{2,0,1:T(8,128)}), f32[59,32,80]{2,0,1:T(8,128)S(1)}, u32[]{:S(2)}, u32[]{:S(2)}) %all-to-all-start) | async-done | bytes 604192 | tf_op jit(solution)/shard_map/all_to_all | solution.py:167
  45.5 583.7 %while.25 = (s32[]{:T(128)}, f32[4,3,32,256]{3,1,2,0:T(4,128)}, s32[4]{0:T(128)}, s32[4,32,512]{2,1,0:T(8,128)}, f32[4,32,256]{2,1,0:T(8,128)}, /*index=5*/f32[4...) while((s32[]{:T(128)}, f32[4,3,32,256]{3,1,2,0:T(4,128)}, ...), condition=%wide.region_9.10_spmd.clone, body=%wide.region_5.9_spmd.clone.sunk | while | flops 1694568448 | bytes 12501576 | solution.py:207
  50.3 139.6 %while.26 = (s32[]{:T(128)}, f32[32,256]{1,0:T(8,128)S(1)}, f32[3,32,256]{2,0,1:T(4,128)}, s32[]{:T(128)}, s32[32,512]{1,0:T(8,128)S(1)}, /*index=5*/f32[9,2560]...) while((s32[]{:T(128)}, f32[32,256]{1,0:T(8,128)S(1)}, ...), condition=%wide.region_8.8_spmd, body=%wide.region_6.7_spmd.sunk | while | flops 1694535680 | bytes 11780395 | solution.py:205
  50.9 10.8 %gather_fusion = f32[4096,9]{1,0:T(8,128)S(1)} fusion(f32[9,2560]{0,1:T(8,128)S(1)} %get-tuple-element.393, s32[4096]{0:T(1024)S(1)} %bitcast_clamp_fusion.2), kind=kCustom, calls=%fused_computation.clone.1 | custom fusion | bytes 311296 | tf_op jit(solution)/shard_map/while/body/eval_jaxpr/while/body/gather | solution.py:191
  72.5 7.7 %fusion.97 = f32[3,32,256]{2,0,1:T(4,128)S(1)} fusion(f32[3,32,256]{2,0,1:T(4,128)S(1)} %copy-done.1, f32[32,256,128]{2,1,0:T(8,128)S(1)} %fusion.96, f32[32,256]{1,0:T(8,128)S(1)} %get-tuple-element.376, f32[32,128]{1,0:T(8,128)S(1)} %bitcast.86, f32[32,128]{1,0:T(8,128)S(1)} %bitcast.89, f32[32,256]{1,0:T(8,128)S(1)} %get-tuple-element.395, ...), kind=kOutput, calls=%fused_computation.24.clone.1 | convolution fusion | flops 53501952 | bytes 4689920 | tf_op jit(solution)/shard_map/while/body/eval_jaxpr/while/body/tpk,ctk->ctp/dot_general | solution.py:196
  85.6 10.8 %gather_fusion = f32[4096,9]{1,0:T(8,128)S(1)} fusion(f32[9,2560]{0,1:T(8,128)S(1)} %get-tuple-element.393, s32[4096]{0:T(1024)S(1)} %bitcast_clamp_fusion.2), kind=kCustom, calls=%fused_computation.clone.1 | custom fusion | bytes 311296 | tf_op jit(solution)/shard_map/while/body/eval_jaxpr/while/body/gather | solution.py:191
  99.6 7.6 %fusion.96 = f32[32,256,128]{2,1,0:T(8,128)S(1)} fusion(f32[32,128]{1,0:T(8,128)S(1)} %bitcast.85, f32[32,128]{1,0:T(8,128)S(1)} %bitcast.88, f32[32,256]{1,0:T(8,128)S(1)} %get-tuple-element.395, f32[32,128]{1,0:T(8,128)S(1)} %bitcast.91, f32[32,128]{1,0:T(8,128)S(1)} %bitcast.94, f32[32,256]{1,0:T(8,128)} %get-tuple-element.394, ...), kind=kOutput, calls=%fused_computation.20.clone.1 | convolution fusion | flops 1625292800 | bytes 4427776 | tf_op jit(solution)/shard_map/while/body/eval_jaxpr/while/body/tpk,kj->tpj/dot_general | solution.py:194
  107.2 7.7 %fusion.97 = f32[3,32,256]{2,0,1:T(4,128)S(1)} fusion(f32[3,32,256]{2,0,1:T(4,128)S(1)} %copy-done.1, f32[32,256,128]{2,1,0:T(8,128)S(1)} %fusion.96, f32[32,256]{1,0:T(8,128)S(1)} %get-tuple-element.376, f32[32,128]{1,0:T(8,128)S(1)} %bitcast.86, f32[32,128]{1,0:T(8,128)S(1)} %bitcast.89, f32[32,256]{1,0:T(8,128)S(1)} %get-tuple-element.395, ...), kind=kOutput, calls=%fused_computation.24.clone.1 | convolution fusion | flops 53501952 | bytes 4689920 | tf_op jit(solution)/shard_map/while/body/eval_jaxpr/while/body/tpk,ctk->ctp/dot_general | solution.py:196
  120.4 10.8 %gather_fusion = f32[4096,9]{1,0:T(8,128)S(1)} fusion(f32[9,2560]{0,1:T(8,128)S(1)} %get-tuple-element.393, s32[4096]{0:T(1024)S(1)} %bitcast_clamp_fusion.2), kind=kCustom, calls=%fused_computation.clone.1 | custom fusion | bytes 311296 | tf_op jit(solution)/shard_map/while/body/eval_jaxpr/while/body/gather | solution.py:191
  134.4 7.6 %fusion.96 = f32[32,256,128]{2,1,0:T(8,128)S(1)} fusion(f32[32,128]{1,0:T(8,128)S(1)} %bitcast.85, f32[32,128]{1,0:T(8,128)S(1)} %bitcast.88, f32[32,256]{1,0:T(8,128)S(1)} %get-tuple-element.395, f32[32,128]{1,0:T(8,128)S(1)} %bitcast.91, f32[32,128]{1,0:T(8,128)S(1)} %bitcast.94, f32[32,256]{1,0:T(8,128)} %get-tuple-element.394, ...), kind=kOutput, calls=%fused_computation.20.clone.1 | convolution fusion | flops 1625292800 | bytes 4427776 | tf_op jit(solution)/shard_map/while/body/eval_jaxpr/while/body/tpk,kj->tpj/dot_general | solution.py:194
  142.0 7.7 %fusion.97 = f32[3,32,256]{2,0,1:T(4,128)S(1)} fusion(f32[3,32,256]{2,0,1:T(4,128)S(1)} %copy-done.1, f32[32,256,128]{2,1,0:T(8,128)S(1)} %fusion.96, f32[32,256]{1,0:T(8,128)S(1)} %get-tuple-element.376, f32[32,128]{1,0:T(8,128)S(1)} %bitcast.86, f32[32,128]{1,0:T(8,128)S(1)} %bitcast.89, f32[32,256]{1,0:T(8,128)S(1)} %get-tuple-element.395, ...), kind=kOutput, calls=%fused_computation.24.clone.1 | convolution fusion | flops 53501952 | bytes 4689920 | tf_op jit(solution)/shard_map/while/body/eval_jaxpr/while/body/tpk,ctk->ctp/dot_general | solution.py:196
  155.2 10.8 %gather_fusion = f32[4096,9]{1,0:T(8,128)S(1)} fusion(f32[9,2560]{0,1:T(8,128)S(1)} %get-tuple-element.393, s32[4096]{0:T(1024)S(1)} %bitcast_clamp_fusion.2), kind=kCustom, calls=%fused_computation.clone.1 | custom fusion | bytes 311296 | tf_op jit(solution)/shard_map/while/body/eval_jaxpr/while/body/gather | solution.py:191
  176.8 7.7 %fusion.97 = f32[3,32,256]{2,0,1:T(4,128)S(1)} fusion(f32[3,32,256]{2,0,1:T(4,128)S(1)} %copy-done.1, f32[32,256,128]{2,1,0:T(8,128)S(1)} %fusion.96, f32[32,256]{1,0:T(8,128)S(1)} %get-tuple-element.376, f32[32,128]{1,0:T(8,128)S(1)} %bitcast.86, f32[32,128]{1,0:T(8,128)S(1)} %bitcast.89, f32[32,256]{1,0:T(8,128)S(1)} %get-tuple-element.395, ...), kind=kOutput, calls=%fused_computation.24.clone.1 | convolution fusion | flops 53501952 | bytes 4689920 | tf_op jit(solution)/shard_map/while/body/eval_jaxpr/while/body/tpk,ctk->ctp/dot_general | solution.py:196
  196.2 139.6 %while.26 = (s32[]{:T(128)}, f32[32,256]{1,0:T(8,128)S(1)}, f32[3,32,256]{2,0,1:T(4,128)}, s32[]{:T(128)}, s32[32,512]{1,0:T(8,128)S(1)}, /*index=5*/f32[9,2560]...) while((s32[]{:T(128)}, f32[32,256]{1,0:T(8,128)S(1)}, ...), condition=%wide.region_8.8_spmd, body=%wide.region_6.7_spmd.sunk | while | flops 1694535680 | bytes 11780395 | solution.py:205
  196.8 10.8 %gather_fusion = f32[4096,9]{1,0:T(8,128)S(1)} fusion(f32[9,2560]{0,1:T(8,128)S(1)} %get-tuple-element.393, s32[4096]{0:T(1024)S(1)} %bitcast_clamp_fusion.2), kind=kCustom, calls=%fused_computation.clone.1 | custom fusion | bytes 311296 | tf_op jit(solution)/shard_map/while/body/eval_jaxpr/while/body/gather | solution.py:191
  210.8 7.6 %fusion.96 = f32[32,256,128]{2,1,0:T(8,128)S(1)} fusion(f32[32,128]{1,0:T(8,128)S(1)} %bitcast.85, f32[32,128]{1,0:T(8,128)S(1)} %bitcast.88, f32[32,256]{1,0:T(8,128)S(1)} %get-tuple-element.395, f32[32,128]{1,0:T(8,128)S(1)} %bitcast.91, f32[32,128]{1,0:T(8,128)S(1)} %bitcast.94, f32[32,256]{1,0:T(8,128)} %get-tuple-element.394, ...), kind=kOutput, calls=%fused_computation.20.clone.1 | convolution fusion | flops 1625292800 | bytes 4427776 | tf_op jit(solution)/shard_map/while/body/eval_jaxpr/while/body/tpk,kj->tpj/dot_general | solution.py:194
  218.4 7.7 %fusion.97 = f32[3,32,256]{2,0,1:T(4,128)S(1)} fusion(f32[3,32,256]{2,0,1:T(4,128)S(1)} %copy-done.1, f32[32,256,128]{2,1,0:T(8,128)S(1)} %fusion.96, f32[32,256]{1,0:T(8,128)S(1)} %get-tuple-element.376, f32[32,128]{1,0:T(8,128)S(1)} %bitcast.86, f32[32,128]{1,0:T(8,128)S(1)} %bitcast.89, f32[32,256]{1,0:T(8,128)S(1)} %get-tuple-element.395, ...), kind=kOutput, calls=%fused_computation.24.clone.1 | convolution fusion | flops 53501952 | bytes 4689920 | tf_op jit(solution)/shard_map/while/body/eval_jaxpr/while/body/tpk,ctk->ctp/dot_general | solution.py:196
  231.6 10.8 %gather_fusion = f32[4096,9]{1,0:T(8,128)S(1)} fusion(f32[9,2560]{0,1:T(8,128)S(1)} %get-tuple-element.393, s32[4096]{0:T(1024)S(1)} %bitcast_clamp_fusion.2), kind=kCustom, calls=%fused_computation.clone.1 | custom fusion | bytes 311296 | tf_op jit(solution)/shard_map/while/body/eval_jaxpr/while/body/gather | solution.py:191
  253.2 7.7 %fusion.97 = f32[3,32,256]{2,0,1:T(4,128)S(1)} fusion(f32[3,32,256]{2,0,1:T(4,128)S(1)} %copy-done.1, f32[32,256,128]{2,1,0:T(8,128)S(1)} %fusion.96, f32[32,256]{1,0:T(8,128)S(1)} %get-tuple-element.376, f32[32,128]{1,0:T(8,128)S(1)} %bitcast.86, f32[32,128]{1,0:T(8,128)S(1)} %bitcast.89, f32[32,256]{1,0:T(8,128)S(1)} %get-tuple-element.395, ...), kind=kOutput, calls=%fused_computation.24.clone.1 | convolution fusion | flops 53501952 | bytes 4689920 | tf_op jit(solution)/shard_map/while/body/eval_jaxpr/while/body/tpk,ctk->ctp/dot_general | solution.py:196
  266.3 10.8 %gather_fusion = f32[4096,9]{1,0:T(8,128)S(1)} fusion(f32[9,2560]{0,1:T(8,128)S(1)} %get-tuple-element.393, s32[4096]{0:T(1024)S(1)} %bitcast_clamp_fusion.2), kind=kCustom, calls=%fused_computation.clone.1 | custom fusion | bytes 311296 | tf_op jit(solution)/shard_map/while/body/eval_jaxpr/while/body/gather | solution.py:191
  280.3 7.6 %fusion.96 = f32[32,256,128]{2,1,0:T(8,128)S(1)} fusion(f32[32,128]{1,0:T(8,128)S(1)} %bitcast.85, f32[32,128]{1,0:T(8,128)S(1)} %bitcast.88, f32[32,256]{1,0:T(8,128)S(1)} %get-tuple-element.395, f32[32,128]{1,0:T(8,128)S(1)} %bitcast.91, f32[32,128]{1,0:T(8,128)S(1)} %bitcast.94, f32[32,256]{1,0:T(8,128)} %get-tuple-element.394, ...), kind=kOutput, calls=%fused_computation.20.clone.1 | convolution fusion | flops 1625292800 | bytes 4427776 | tf_op jit(solution)/shard_map/while/body/eval_jaxpr/while/body/tpk,kj->tpj/dot_general | solution.py:194
  287.9 7.7 %fusion.97 = f32[3,32,256]{2,0,1:T(4,128)S(1)} fusion(f32[3,32,256]{2,0,1:T(4,128)S(1)} %copy-done.1, f32[32,256,128]{2,1,0:T(8,128)S(1)} %fusion.96, f32[32,256]{1,0:T(8,128)S(1)} %get-tuple-element.376, f32[32,128]{1,0:T(8,128)S(1)} %bitcast.86, f32[32,128]{1,0:T(8,128)S(1)} %bitcast.89, f32[32,256]{1,0:T(8,128)S(1)} %get-tuple-element.395, ...), kind=kOutput, calls=%fused_computation.24.clone.1 | convolution fusion | flops 53501952 | bytes 4689920 | tf_op jit(solution)/shard_map/while/body/eval_jaxpr/while/body/tpk,ctk->ctp/dot_general | solution.py:196
  301.1 10.8 %gather_fusion = f32[4096,9]{1,0:T(8,128)S(1)} fusion(f32[9,2560]{0,1:T(8,128)S(1)} %get-tuple-element.393, s32[4096]{0:T(1024)S(1)} %bitcast_clamp_fusion.2), kind=kCustom, calls=%fused_computation.clone.1 | custom fusion | bytes 311296 | tf_op jit(solution)/shard_map/while/body/eval_jaxpr/while/body/gather | solution.py:191
  322.7 7.7 %fusion.97 = f32[3,32,256]{2,0,1:T(4,128)S(1)} fusion(f32[3,32,256]{2,0,1:T(4,128)S(1)} %copy-done.1, f32[32,256,128]{2,1,0:T(8,128)S(1)} %fusion.96, f32[32,256]{1,0:T(8,128)S(1)} %get-tuple-element.376, f32[32,128]{1,0:T(8,128)S(1)} %bitcast.86, f32[32,128]{1,0:T(8,128)S(1)} %bitcast.89, f32[32,256]{1,0:T(8,128)S(1)} %get-tuple-element.395, ...), kind=kOutput, calls=%fused_computation.24.clone.1 | convolution fusion | flops 53501952 | bytes 4689920 | tf_op jit(solution)/shard_map/while/body/eval_jaxpr/while/body/tpk,ctk->ctp/dot_general | solution.py:196
  342.1 139.6 %while.26 = (s32[]{:T(128)}, f32[32,256]{1,0:T(8,128)S(1)}, f32[3,32,256]{2,0,1:T(4,128)}, s32[]{:T(128)}, s32[32,512]{1,0:T(8,128)S(1)}, /*index=5*/f32[9,2560]...) while((s32[]{:T(128)}, f32[32,256]{1,0:T(8,128)S(1)}, ...), condition=%wide.region_8.8_spmd, body=%wide.region_6.7_spmd.sunk | while | flops 1694535680 | bytes 11780395 | solution.py:205
  342.7 10.8 %gather_fusion = f32[4096,9]{1,0:T(8,128)S(1)} fusion(f32[9,2560]{0,1:T(8,128)S(1)} %get-tuple-element.393, s32[4096]{0:T(1024)S(1)} %bitcast_clamp_fusion.2), kind=kCustom, calls=%fused_computation.clone.1 | custom fusion | bytes 311296 | tf_op jit(solution)/shard_map/while/body/eval_jaxpr/while/body/gather | solution.py:191
  356.7 7.6 %fusion.96 = f32[32,256,128]{2,1,0:T(8,128)S(1)} fusion(f32[32,128]{1,0:T(8,128)S(1)} %bitcast.85, f32[32,128]{1,0:T(8,128)S(1)} %bitcast.88, f32[32,256]{1,0:T(8,128)S(1)} %get-tuple-element.395, f32[32,128]{1,0:T(8,128)S(1)} %bitcast.91, f32[32,128]{1,0:T(8,128)S(1)} %bitcast.94, f32[32,256]{1,0:T(8,128)} %get-tuple-element.394, ...), kind=kOutput, calls=%fused_computation.20.clone.1 | convolution fusion | flops 1625292800 | bytes 4427776 | tf_op jit(solution)/shard_map/while/body/eval_jaxpr/while/body/tpk,kj->tpj/dot_general | solution.py:194
  364.3 7.7 %fusion.97 = f32[3,32,256]{2,0,1:T(4,128)S(1)} fusion(f32[3,32,256]{2,0,1:T(4,128)S(1)} %copy-done.1, f32[32,256,128]{2,1,0:T(8,128)S(1)} %fusion.96, f32[32,256]{1,0:T(8,128)S(1)} %get-tuple-element.376, f32[32,128]{1,0:T(8,128)S(1)} %bitcast.86, f32[32,128]{1,0:T(8,128)S(1)} %bitcast.89, f32[32,256]{1,0:T(8,128)S(1)} %get-tuple-element.395, ...), kind=kOutput, calls=%fused_computation.24.clone.1 | convolution fusion | flops 53501952 | bytes 4689920 | tf_op jit(solution)/shard_map/while/body/eval_jaxpr/while/body/tpk,ctk->ctp/dot_general | solution.py:196
  377.5 10.8 %gather_fusion = f32[4096,9]{1,0:T(8,128)S(1)} fusion(f32[9,2560]{0,1:T(8,128)S(1)} %get-tuple-element.393, s32[4096]{0:T(1024)S(1)} %bitcast_clamp_fusion.2), kind=kCustom, calls=%fused_computation.clone.1 | custom fusion | bytes 311296 | tf_op jit(solution)/shard_map/while/body/eval_jaxpr/while/body/gather | solution.py:191
  391.5 7.6 %fusion.96 = f32[32,256,128]{2,1,0:T(8,128)S(1)} fusion(f32[32,128]{1,0:T(8,128)S(1)} %bitcast.85, f32[32,128]{1,0:T(8,128)S(1)} %bitcast.88, f32[32,256]{1,0:T(8,128)S(1)} %get-tuple-element.395, f32[32,128]{1,0:T(8,128)S(1)} %bitcast.91, f32[32,128]{1,0:T(8,128)S(1)} %bitcast.94, f32[32,256]{1,0:T(8,128)} %get-tuple-element.394, ...), kind=kOutput, calls=%fused_computation.20.clone.1 | convolution fusion | flops 1625292800 | bytes 4427776 | tf_op jit(solution)/shard_map/while/body/eval_jaxpr/while/body/tpk,kj->tpj/dot_general | solution.py:194
  399.1 7.7 %fusion.97 = f32[3,32,256]{2,0,1:T(4,128)S(1)} fusion(f32[3,32,256]{2,0,1:T(4,128)S(1)} %copy-done.1, f32[32,256,128]{2,1,0:T(8,128)S(1)} %fusion.96, f32[32,256]{1,0:T(8,128)S(1)} %get-tuple-element.376, f32[32,128]{1,0:T(8,128)S(1)} %bitcast.86, f32[32,128]{1,0:T(8,128)S(1)} %bitcast.89, f32[32,256]{1,0:T(8,128)S(1)} %get-tuple-element.395, ...), kind=kOutput, calls=%fused_computation.24.clone.1 | convolution fusion | flops 53501952 | bytes 4689920 | tf_op jit(solution)/shard_map/while/body/eval_jaxpr/while/body/tpk,ctk->ctp/dot_general | solution.py:196
  412.3 10.8 %gather_fusion = f32[4096,9]{1,0:T(8,128)S(1)} fusion(f32[9,2560]{0,1:T(8,128)S(1)} %get-tuple-element.393, s32[4096]{0:T(1024)S(1)} %bitcast_clamp_fusion.2), kind=kCustom, calls=%fused_computation.clone.1 | custom fusion | bytes 311296 | tf_op jit(solution)/shard_map/while/body/eval_jaxpr/while/body/gather | solution.py:191
  426.2 7.6 %fusion.96 = f32[32,256,128]{2,1,0:T(8,128)S(1)} fusion(f32[32,128]{1,0:T(8,128)S(1)} %bitcast.85, f32[32,128]{1,0:T(8,128)S(1)} %bitcast.88, f32[32,256]{1,0:T(8,128)S(1)} %get-tuple-element.395, f32[32,128]{1,0:T(8,128)S(1)} %bitcast.91, f32[32,128]{1,0:T(8,128)S(1)} %bitcast.94, f32[32,256]{1,0:T(8,128)} %get-tuple-element.394, ...), kind=kOutput, calls=%fused_computation.20.clone.1 | convolution fusion | flops 1625292800 | bytes 4427776 | tf_op jit(solution)/shard_map/while/body/eval_jaxpr/while/body/tpk,kj->tpj/dot_general | solution.py:194
  433.9 7.7 %fusion.97 = f32[3,32,256]{2,0,1:T(4,128)S(1)} fusion(f32[3,32,256]{2,0,1:T(4,128)S(1)} %copy-done.1, f32[32,256,128]{2,1,0:T(8,128)S(1)} %fusion.96, f32[32,256]{1,0:T(8,128)S(1)} %get-tuple-element.376, f32[32,128]{1,0:T(8,128)S(1)} %bitcast.86, f32[32,128]{1,0:T(8,128)S(1)} %bitcast.89, f32[32,256]{1,0:T(8,128)S(1)} %get-tuple-element.395, ...), kind=kOutput, calls=%fused_computation.24.clone.1 | convolution fusion | flops 53501952 | bytes 4689920 | tf_op jit(solution)/shard_map/while/body/eval_jaxpr/while/body/tpk,ctk->ctp/dot_general | solution.py:196
  447.0 10.8 %gather_fusion = f32[4096,9]{1,0:T(8,128)S(1)} fusion(f32[9,2560]{0,1:T(8,128)S(1)} %get-tuple-element.393, s32[4096]{0:T(1024)S(1)} %bitcast_clamp_fusion.2), kind=kCustom, calls=%fused_computation.clone.1 | custom fusion | bytes 311296 | tf_op jit(solution)/shard_map/while/body/eval_jaxpr/while/body/gather | solution.py:191
  461.0 7.6 %fusion.96 = f32[32,256,128]{2,1,0:T(8,128)S(1)} fusion(f32[32,128]{1,0:T(8,128)S(1)} %bitcast.85, f32[32,128]{1,0:T(8,128)S(1)} %bitcast.88, f32[32,256]{1,0:T(8,128)S(1)} %get-tuple-element.395, f32[32,128]{1,0:T(8,128)S(1)} %bitcast.91, f32[32,128]{1,0:T(8,128)S(1)} %bitcast.94, f32[32,256]{1,0:T(8,128)} %get-tuple-element.394, ...), kind=kOutput, calls=%fused_computation.20.clone.1 | convolution fusion | flops 1625292800 | bytes 4427776 | tf_op jit(solution)/shard_map/while/body/eval_jaxpr/while/body/tpk,kj->tpj/dot_general | solution.py:194
  468.6 7.7 %fusion.97 = f32[3,32,256]{2,0,1:T(4,128)S(1)} fusion(f32[3,32,256]{2,0,1:T(4,128)S(1)} %copy-done.1, f32[32,256,128]{2,1,0:T(8,128)S(1)} %fusion.96, f32[32,256]{1,0:T(8,128)S(1)} %get-tuple-element.376, f32[32,128]{1,0:T(8,128)S(1)} %bitcast.86, f32[32,128]{1,0:T(8,128)S(1)} %bitcast.89, f32[32,256]{1,0:T(8,128)S(1)} %get-tuple-element.395, ...), kind=kOutput, calls=%fused_computation.24.clone.1 | convolution fusion | flops 53501952 | bytes 4689920 | tf_op jit(solution)/shard_map/while/body/eval_jaxpr/while/body/tpk,ctk->ctp/dot_general | solution.py:196
  488.1 139.6 %while.26 = (s32[]{:T(128)}, f32[32,256]{1,0:T(8,128)S(1)}, f32[3,32,256]{2,0,1:T(4,128)}, s32[]{:T(128)}, s32[32,512]{1,0:T(8,128)S(1)}, /*index=5*/f32[9,2560]...) while((s32[]{:T(128)}, f32[32,256]{1,0:T(8,128)S(1)}, ...), condition=%wide.region_8.8_spmd, body=%wide.region_6.7_spmd.sunk | while | flops 1694535680 | bytes 11780395 | solution.py:205
  488.7 10.8 %gather_fusion = f32[4096,9]{1,0:T(8,128)S(1)} fusion(f32[9,2560]{0,1:T(8,128)S(1)} %get-tuple-element.393, s32[4096]{0:T(1024)S(1)} %bitcast_clamp_fusion.2), kind=kCustom, calls=%fused_computation.clone.1 | custom fusion | bytes 311296 | tf_op jit(solution)/shard_map/while/body/eval_jaxpr/while/body/gather | solution.py:191
  510.3 7.7 %fusion.97 = f32[3,32,256]{2,0,1:T(4,128)S(1)} fusion(f32[3,32,256]{2,0,1:T(4,128)S(1)} %copy-done.1, f32[32,256,128]{2,1,0:T(8,128)S(1)} %fusion.96, f32[32,256]{1,0:T(8,128)S(1)} %get-tuple-element.376, f32[32,128]{1,0:T(8,128)S(1)} %bitcast.86, f32[32,128]{1,0:T(8,128)S(1)} %bitcast.89, f32[32,256]{1,0:T(8,128)S(1)} %get-tuple-element.395, ...), kind=kOutput, calls=%fused_computation.24.clone.1 | convolution fusion | flops 53501952 | bytes 4689920 | tf_op jit(solution)/shard_map/while/body/eval_jaxpr/while/body/tpk,ctk->ctp/dot_general | solution.py:196
  523.4 10.8 %gather_fusion = f32[4096,9]{1,0:T(8,128)S(1)} fusion(f32[9,2560]{0,1:T(8,128)S(1)} %get-tuple-element.393, s32[4096]{0:T(1024)S(1)} %bitcast_clamp_fusion.2), kind=kCustom, calls=%fused_computation.clone.1 | custom fusion | bytes 311296 | tf_op jit(solution)/shard_map/while/body/eval_jaxpr/while/body/gather | solution.py:191
  545.0 7.7 %fusion.97 = f32[3,32,256]{2,0,1:T(4,128)S(1)} fusion(f32[3,32,256]{2,0,1:T(4,128)S(1)} %copy-done.1, f32[32,256,128]{2,1,0:T(8,128)S(1)} %fusion.96, f32[32,256]{1,0:T(8,128)S(1)} %get-tuple-element.376, f32[32,128]{1,0:T(8,128)S(1)} %bitcast.86, f32[32,128]{1,0:T(8,128)S(1)} %bitcast.89, f32[32,256]{1,0:T(8,128)S(1)} %get-tuple-element.395, ...), kind=kOutput, calls=%fused_computation.24.clone.1 | convolution fusion | flops 53501952 | bytes 4689920 | tf_op jit(solution)/shard_map/while/body/eval_jaxpr/while/body/tpk,ctk->ctp/dot_general | solution.py:196
  558.2 10.8 %gather_fusion = f32[4096,9]{1,0:T(8,128)S(1)} fusion(f32[9,2560]{0,1:T(8,128)S(1)} %get-tuple-element.393, s32[4096]{0:T(1024)S(1)} %bitcast_clamp_fusion.2), kind=kCustom, calls=%fused_computation.clone.1 | custom fusion | bytes 311296 | tf_op jit(solution)/shard_map/while/body/eval_jaxpr/while/body/gather | solution.py:191
  579.8 7.7 %fusion.97 = f32[3,32,256]{2,0,1:T(4,128)S(1)} fusion(f32[3,32,256]{2,0,1:T(4,128)S(1)} %copy-done.1, f32[32,256,128]{2,1,0:T(8,128)S(1)} %fusion.96, f32[32,256]{1,0:T(8,128)S(1)} %get-tuple-element.376, f32[32,128]{1,0:T(8,128)S(1)} %bitcast.86, f32[32,128]{1,0:T(8,128)S(1)} %bitcast.89, f32[32,256]{1,0:T(8,128)S(1)} %get-tuple-element.395, ...), kind=kOutput, calls=%fused_computation.24.clone.1 | convolution fusion | flops 53501952 | bytes 4689920 | tf_op jit(solution)/shard_map/while/body/eval_jaxpr/while/body/tpk,ctk->ctp/dot_general | solution.py:196
  593.0 10.8 %gather_fusion = f32[4096,9]{1,0:T(8,128)S(1)} fusion(f32[9,2560]{0,1:T(8,128)S(1)} %get-tuple-element.393, s32[4096]{0:T(1024)S(1)} %bitcast_clamp_fusion.2), kind=kCustom, calls=%fused_computation.clone.1 | custom fusion | bytes 311296 | tf_op jit(solution)/shard_map/while/body/eval_jaxpr/while/body/gather | solution.py:191
  614.6 7.7 %fusion.97 = f32[3,32,256]{2,0,1:T(4,128)S(1)} fusion(f32[3,32,256]{2,0,1:T(4,128)S(1)} %copy-done.1, f32[32,256,128]{2,1,0:T(8,128)S(1)} %fusion.96, f32[32,256]{1,0:T(8,128)S(1)} %get-tuple-element.376, f32[32,128]{1,0:T(8,128)S(1)} %bitcast.86, f32[32,128]{1,0:T(8,128)S(1)} %bitcast.89, f32[32,256]{1,0:T(8,128)S(1)} %get-tuple-element.395, ...), kind=kOutput, calls=%fused_computation.24.clone.1 | convolution fusion | flops 53501952 | bytes 4689920 | tf_op jit(solution)/shard_map/while/body/eval_jaxpr/while/body/tpk,ctk->ctp/dot_general | solution.py:196
  649.5 8.5 %collective-permute-done = f32[6,128,5]{2,1,0:T(8,128)S(1)} collective-permute-done((f32[6,128,5]{2,1,0:T(8,128)S(1)}, f32[6,128,5]{2,1,0:T(8,128)S(1)}, u32[]{:S(2)}, u32[]{:S(2)}) %collective-permute-start) | collective-permute-done | bytes 15392 | tf_op jit(solution)/shard_map/ppermute | solution.py:40
  664.1 8.6 %fusion.30 = f32[15,266,128]{2,1,0:T(8,128)S(1)} fusion(f32[3,138,266]{2,1,0:T(8,128)S(1)} %get-tuple-element.199, f32[3,138,266]{2,1,0:T(8,128)S(1)} %get-tuple-element.200, f32[3,138,266]{2,1,0:T(8,128)S(1)} %get-tuple-element.198, f32[6,5,266]{2,1,0:T(8,128)S(1)} %collective-permute-done.3, f32[6,128,5]{2,1,0:T(8,128)S(1)} %collective-permute-done.1, ...), kind=kOutput, calls=%fused_computation.39 | convolution fusion | flops 849606656 | bytes 4316016 | tf_op jit(solution)/shard_map/ij,cjw->ciw/dot_general | solution.py:229
  (346 shorter events, 270.6 us)
Async XLA Ops:
  8.2 33.5 %all-to-all-start = ((f32[59,32,80]{2,0,1:T(8,128)}), f32[59,32,80]{2,0,1:T(8,128)S(1)}, u32[]{:S(2)}, u32[]{:S(2)}) async-start(f32[59,32,80]{2,0,1:T(8,128)} %copy.59), calls=%async_computation | async-start | bytes 2097152 | tf_op jit(solution)/shard_map/all_to_all | solution.py:167
  64.8 7.6 %copy-start = (f32[32,128,9]{1,2,0:T(8,128)S(1)}, f32[32,128,9]{1,2,0:T(8,128)}, u32[]{:S(2)}) copy-start(f32[32,128,9]{1,2,0:T(8,128)} %copy.71) | copy-start | bytes 442372 | tf_op jit(solution)/shard_map/while/body/eval_jaxpr/while
  99.6 7.6 %copy-start = (f32[32,128,9]{1,2,0:T(8,128)S(1)}, f32[32,128,9]{1,2,0:T(8,128)}, u32[]{:S(2)}) copy-start(f32[32,128,9]{1,2,0:T(8,128)} %copy.71) | copy-start | bytes 442372 | tf_op jit(solution)/shard_map/while/body/eval_jaxpr/while
  99.6 7.6 %copy-start.1 = (f32[3,32,256]{2,0,1:T(4,128)S(1)}, f32[3,32,256]{2,0,1:T(4,128)}, u32[]{:S(2)}) copy-start(f32[3,32,256]{2,0,1:T(4,128)} %get-tuple-element.377) | copy-start | bytes 294916 | tf_op jit(solution)/shard_map/while/body/eval_jaxpr/while
  99.6 7.6 %copy-start.5 = (f32[32,256]{1,0:T(8,128)S(1)}, f32[32,256]{1,0:T(8,128)}, u32[]{:S(2)}) copy-start(f32[32,256]{1,0:T(8,128)} %get-tuple-element.394) | copy-start | bytes 98308 | tf_op jit(solution)/shard_map/while/body/eval_jaxpr/while
  134.3 7.6 %copy-start = (f32[32,128,9]{1,2,0:T(8,128)S(1)}, f32[32,128,9]{1,2,0:T(8,128)}, u32[]{:S(2)}) copy-start(f32[32,128,9]{1,2,0:T(8,128)} %copy.71) | copy-start | bytes 442372 | tf_op jit(solution)/shard_map/while/body/eval_jaxpr/while
  134.4 7.6 %copy-start.1 = (f32[3,32,256]{2,0,1:T(4,128)S(1)}, f32[3,32,256]{2,0,1:T(4,128)}, u32[]{:S(2)}) copy-start(f32[3,32,256]{2,0,1:T(4,128)} %get-tuple-element.377) | copy-start | bytes 294916 | tf_op jit(solution)/shard_map/while/body/eval_jaxpr/while
  134.4 7.6 %copy-start.5 = (f32[32,256]{1,0:T(8,128)S(1)}, f32[32,256]{1,0:T(8,128)}, u32[]{:S(2)}) copy-start(f32[32,256]{1,0:T(8,128)} %get-tuple-element.394) | copy-start | bytes 98308 | tf_op jit(solution)/shard_map/while/body/eval_jaxpr/while
  169.1 7.6 %copy-start = (f32[32,128,9]{1,2,0:T(8,128)S(1)}, f32[32,128,9]{1,2,0:T(8,128)}, u32[]{:S(2)}) copy-start(f32[32,128,9]{1,2,0:T(8,128)} %copy.71) | copy-start | bytes 442372 | tf_op jit(solution)/shard_map/while/body/eval_jaxpr/while
  210.7 7.6 %copy-start = (f32[32,128,9]{1,2,0:T(8,128)S(1)}, f32[32,128,9]{1,2,0:T(8,128)}, u32[]{:S(2)}) copy-start(f32[32,128,9]{1,2,0:T(8,128)} %copy.71) | copy-start | bytes 442372 | tf_op jit(solution)/shard_map/while/body/eval_jaxpr/while
  210.8 7.6 %copy-start.1 = (f32[3,32,256]{2,0,1:T(4,128)S(1)}, f32[3,32,256]{2,0,1:T(4,128)}, u32[]{:S(2)}) copy-start(f32[3,32,256]{2,0,1:T(4,128)} %get-tuple-element.377) | copy-start | bytes 294916 | tf_op jit(solution)/shard_map/while/body/eval_jaxpr/while
  210.8 7.6 %copy-start.5 = (f32[32,256]{1,0:T(8,128)S(1)}, f32[32,256]{1,0:T(8,128)}, u32[]{:S(2)}) copy-start(f32[32,256]{1,0:T(8,128)} %get-tuple-element.394) | copy-start | bytes 98308 | tf_op jit(solution)/shard_map/while/body/eval_jaxpr/while
  245.5 7.6 %copy-start = (f32[32,128,9]{1,2,0:T(8,128)S(1)}, f32[32,128,9]{1,2,0:T(8,128)}, u32[]{:S(2)}) copy-start(f32[32,128,9]{1,2,0:T(8,128)} %copy.71) | copy-start | bytes 442372 | tf_op jit(solution)/shard_map/while/body/eval_jaxpr/while
  245.5 7.6 %copy-start.1 = (f32[3,32,256]{2,0,1:T(4,128)S(1)}, f32[3,32,256]{2,0,1:T(4,128)}, u32[]{:S(2)}) copy-start(f32[3,32,256]{2,0,1:T(4,128)} %get-tuple-element.377) | copy-start | bytes 294916 | tf_op jit(solution)/shard_map/while/body/eval_jaxpr/while
  245.5 7.6 %copy-start.5 = (f32[32,256]{1,0:T(8,128)S(1)}, f32[32,256]{1,0:T(8,128)}, u32[]{:S(2)}) copy-start(f32[32,256]{1,0:T(8,128)} %get-tuple-element.394) | copy-start | bytes 98308 | tf_op jit(solution)/shard_map/while/body/eval_jaxpr/while
  280.3 7.6 %copy-start = (f32[32,128,9]{1,2,0:T(8,128)S(1)}, f32[32,128,9]{1,2,0:T(8,128)}, u32[]{:S(2)}) copy-start(f32[32,128,9]{1,2,0:T(8,128)} %copy.71) | copy-start | bytes 442372 | tf_op jit(solution)/shard_map/while/body/eval_jaxpr/while
  280.3 7.6 %copy-start.1 = (f32[3,32,256]{2,0,1:T(4,128)S(1)}, f32[3,32,256]{2,0,1:T(4,128)}, u32[]{:S(2)}) copy-start(f32[3,32,256]{2,0,1:T(4,128)} %get-tuple-element.377) | copy-start | bytes 294916 | tf_op jit(solution)/shard_map/while/body/eval_jaxpr/while
  280.3 7.6 %copy-start.5 = (f32[32,256]{1,0:T(8,128)S(1)}, f32[32,256]{1,0:T(8,128)}, u32[]{:S(2)}) copy-start(f32[32,256]{1,0:T(8,128)} %get-tuple-element.394) | copy-start | bytes 98308 | tf_op jit(solution)/shard_map/while/body/eval_jaxpr/while
  315.0 7.6 %copy-start = (f32[32,128,9]{1,2,0:T(8,128)S(1)}, f32[32,128,9]{1,2,0:T(8,128)}, u32[]{:S(2)}) copy-start(f32[32,128,9]{1,2,0:T(8,128)} %copy.71) | copy-start | bytes 442372 | tf_op jit(solution)/shard_map/while/body/eval_jaxpr/while
  356.7 7.6 %copy-start = (f32[32,128,9]{1,2,0:T(8,128)S(1)}, f32[32,128,9]{1,2,0:T(8,128)}, u32[]{:S(2)}) copy-start(f32[32,128,9]{1,2,0:T(8,128)} %copy.71) | copy-start | bytes 442372 | tf_op jit(solution)/shard_map/while/body/eval_jaxpr/while
  356.7 7.6 %copy-start.1 = (f32[3,32,256]{2,0,1:T(4,128)S(1)}, f32[3,32,256]{2,0,1:T(4,128)}, u32[]{:S(2)}) copy-start(f32[3,32,256]{2,0,1:T(4,128)} %get-tuple-element.377) | copy-start | bytes 294916 | tf_op jit(solution)/shard_map/while/body/eval_jaxpr/while
  356.7 7.6 %copy-start.5 = (f32[32,256]{1,0:T(8,128)S(1)}, f32[32,256]{1,0:T(8,128)}, u32[]{:S(2)}) copy-start(f32[32,256]{1,0:T(8,128)} %get-tuple-element.394) | copy-start | bytes 98308 | tf_op jit(solution)/shard_map/while/body/eval_jaxpr/while
  391.4 7.6 %copy-start = (f32[32,128,9]{1,2,0:T(8,128)S(1)}, f32[32,128,9]{1,2,0:T(8,128)}, u32[]{:S(2)}) copy-start(f32[32,128,9]{1,2,0:T(8,128)} %copy.71) | copy-start | bytes 442372 | tf_op jit(solution)/shard_map/while/body/eval_jaxpr/while
  391.5 7.6 %copy-start.1 = (f32[3,32,256]{2,0,1:T(4,128)S(1)}, f32[3,32,256]{2,0,1:T(4,128)}, u32[]{:S(2)}) copy-start(f32[3,32,256]{2,0,1:T(4,128)} %get-tuple-element.377) | copy-start | bytes 294916 | tf_op jit(solution)/shard_map/while/body/eval_jaxpr/while
  391.5 7.6 %copy-start.5 = (f32[32,256]{1,0:T(8,128)S(1)}, f32[32,256]{1,0:T(8,128)}, u32[]{:S(2)}) copy-start(f32[32,256]{1,0:T(8,128)} %get-tuple-element.394) | copy-start | bytes 98308 | tf_op jit(solution)/shard_map/while/body/eval_jaxpr/while
  426.2 7.6 %copy-start = (f32[32,128,9]{1,2,0:T(8,128)S(1)}, f32[32,128,9]{1,2,0:T(8,128)}, u32[]{:S(2)}) copy-start(f32[32,128,9]{1,2,0:T(8,128)} %copy.71) | copy-start | bytes 442372 | tf_op jit(solution)/shard_map/while/body/eval_jaxpr/while
  426.2 7.6 %copy-start.1 = (f32[3,32,256]{2,0,1:T(4,128)S(1)}, f32[3,32,256]{2,0,1:T(4,128)}, u32[]{:S(2)}) copy-start(f32[3,32,256]{2,0,1:T(4,128)} %get-tuple-element.377) | copy-start | bytes 294916 | tf_op jit(solution)/shard_map/while/body/eval_jaxpr/while
  426.2 7.6 %copy-start.5 = (f32[32,256]{1,0:T(8,128)S(1)}, f32[32,256]{1,0:T(8,128)}, u32[]{:S(2)}) copy-start(f32[32,256]{1,0:T(8,128)} %get-tuple-element.394) | copy-start | bytes 98308 | tf_op jit(solution)/shard_map/while/body/eval_jaxpr/while
  461.0 7.6 %copy-start = (f32[32,128,9]{1,2,0:T(8,128)S(1)}, f32[32,128,9]{1,2,0:T(8,128)}, u32[]{:S(2)}) copy-start(f32[32,128,9]{1,2,0:T(8,128)} %copy.71) | copy-start | bytes 442372 | tf_op jit(solution)/shard_map/while/body/eval_jaxpr/while
  461.0 7.6 %copy-start.1 = (f32[3,32,256]{2,0,1:T(4,128)S(1)}, f32[3,32,256]{2,0,1:T(4,128)}, u32[]{:S(2)}) copy-start(f32[3,32,256]{2,0,1:T(4,128)} %get-tuple-element.377) | copy-start | bytes 294916 | tf_op jit(solution)/shard_map/while/body/eval_jaxpr/while
  461.0 7.6 %copy-start.5 = (f32[32,256]{1,0:T(8,128)S(1)}, f32[32,256]{1,0:T(8,128)}, u32[]{:S(2)}) copy-start(f32[32,256]{1,0:T(8,128)} %get-tuple-element.394) | copy-start | bytes 98308 | tf_op jit(solution)/shard_map/while/body/eval_jaxpr/while
  502.6 7.6 %copy-start = (f32[32,128,9]{1,2,0:T(8,128)S(1)}, f32[32,128,9]{1,2,0:T(8,128)}, u32[]{:S(2)}) copy-start(f32[32,128,9]{1,2,0:T(8,128)} %copy.71) | copy-start | bytes 442372 | tf_op jit(solution)/shard_map/while/body/eval_jaxpr/while
  537.4 7.6 %copy-start = (f32[32,128,9]{1,2,0:T(8,128)S(1)}, f32[32,128,9]{1,2,0:T(8,128)}, u32[]{:S(2)}) copy-start(f32[32,128,9]{1,2,0:T(8,128)} %copy.71) | copy-start | bytes 442372 | tf_op jit(solution)/shard_map/while/body/eval_jaxpr/while
  537.4 7.6 %copy-start.1 = (f32[3,32,256]{2,0,1:T(4,128)S(1)}, f32[3,32,256]{2,0,1:T(4,128)}, u32[]{:S(2)}) copy-start(f32[3,32,256]{2,0,1:T(4,128)} %get-tuple-element.377) | copy-start | bytes 294916 | tf_op jit(solution)/shard_map/while/body/eval_jaxpr/while
  537.4 7.6 %copy-start.5 = (f32[32,256]{1,0:T(8,128)S(1)}, f32[32,256]{1,0:T(8,128)}, u32[]{:S(2)}) copy-start(f32[32,256]{1,0:T(8,128)} %get-tuple-element.394) | copy-start | bytes 98308 | tf_op jit(solution)/shard_map/while/body/eval_jaxpr/while
  572.1 7.6 %copy-start = (f32[32,128,9]{1,2,0:T(8,128)S(1)}, f32[32,128,9]{1,2,0:T(8,128)}, u32[]{:S(2)}) copy-start(f32[32,128,9]{1,2,0:T(8,128)} %copy.71) | copy-start | bytes 442372 | tf_op jit(solution)/shard_map/while/body/eval_jaxpr/while
  572.1 7.6 %copy-start.1 = (f32[3,32,256]{2,0,1:T(4,128)S(1)}, f32[3,32,256]{2,0,1:T(4,128)}, u32[]{:S(2)}) copy-start(f32[3,32,256]{2,0,1:T(4,128)} %get-tuple-element.377) | copy-start | bytes 294916 | tf_op jit(solution)/shard_map/while/body/eval_jaxpr/while
  572.2 7.6 %copy-start.5 = (f32[32,256]{1,0:T(8,128)S(1)}, f32[32,256]{1,0:T(8,128)}, u32[]{:S(2)}) copy-start(f32[32,256]{1,0:T(8,128)} %get-tuple-element.394) | copy-start | bytes 98308 | tf_op jit(solution)/shard_map/while/body/eval_jaxpr/while
  606.9 7.6 %copy-start = (f32[32,128,9]{1,2,0:T(8,128)S(1)}, f32[32,128,9]{1,2,0:T(8,128)}, u32[]{:S(2)}) copy-start(f32[32,128,9]{1,2,0:T(8,128)} %copy.71) | copy-start | bytes 442372 | tf_op jit(solution)/shard_map/while/body/eval_jaxpr/while
  606.9 7.6 %copy-start.1 = (f32[3,32,256]{2,0,1:T(4,128)S(1)}, f32[3,32,256]{2,0,1:T(4,128)}, u32[]{:S(2)}) copy-start(f32[3,32,256]{2,0,1:T(4,128)} %get-tuple-element.377) | copy-start | bytes 294916 | tf_op jit(solution)/shard_map/while/body/eval_jaxpr/while
  606.9 7.6 %copy-start.5 = (f32[32,256]{1,0:T(8,128)S(1)}, f32[32,256]{1,0:T(8,128)}, u32[]{:S(2)}) copy-start(f32[32,256]{1,0:T(8,128)} %get-tuple-element.394) | copy-start | bytes 98308 | tf_op jit(solution)/shard_map/while/body/eval_jaxpr/while
  634.2 28.3 %copy-start.8 = (f32[11]{0:T(128)S(1)}, f32[11]{0:T(128)}, u32[]{:S(2)}) copy-start(f32[11]{0:T(128)} %copy-done.7) | copy-start | bytes 136
  637.1 26.9 %copy-start.3 = (f32[3,128,256]{2,1,0:T(8,128)}, f32[3,128,256]{2,1,0:T(8,128)S(1)}, u32[]{:S(2)}) copy-start(f32[3,128,256]{2,1,0:T(8,128)S(1)} %reshape.638) | copy-start | bytes 1179652
  637.4 12.2 %collective-permute-start.1 = (f32[6,128,5]{2,1,0:T(8,128)S(1)}, f32[6,128,5]{2,1,0:T(8,128)S(1)}, u32[]{:S(2)}, u32[]{:S(2)}) collective-permute-start(f32[6,128,5]{2,1,0:T(8,128)S(1)} %get-tuple-element.205), channel_id=1, source_target_pairs={{4,0},{8,4},{12,8},{16,12},{20,16},{24,20},{28,24},{5,1},{9,5},{13... | collective-permute-start | bytes 46088 | tf_op jit(solution)/shard_map/ppermute | solution.py:41
  638.7 19.4 %collective-permute-start = (f32[6,128,5]{2,1,0:T(8,128)S(1)}, f32[6,128,5]{2,1,0:T(8,128)S(1)}, u32[]{:S(2)}, u32[]{:S(2)}) collective-permute-start(f32[6,128,5]{2,1,0:T(8,128)S(1)} %get-tuple-element.204), channel_id=1, source_target_pairs={{0,4},{4,8},{8,12},{12,16},{16,20},{20,24},{24,28},{1,5},{5,9},{9,... | collective-permute-start | bytes 46088 | tf_op jit(solution)/shard_map/ppermute | solution.py:40
  658.2 4.5 collective-permute-start.3
  659.5 3.9 collective-permute-start.2
  664.1 8.6 %copy-start.4 = (f32[256,266]{0,1:T(8,128)S(1)}, f32[256,266]{0,1:T(8,128)}, u32[]{:S(2)}) copy-start(f32[256,266]{0,1:T(8,128)} %select_reduce_fusion) | copy-start | bytes 817156
  (26 other events, 146.2 us)
where the time goes:
time: 683 us; the launch traced here: 679 us
  local copies, waits for them, and re-layouts  263 us (39%)
  matrix products  258 us (38%)
  other arithmetic  89.6 us (13%)
  waiting for transfers between devices  36.4 us (5%)
  starting transfers between devices  17.5 us (3%)
  loops' own time  13.5 us (2%)
    gather x32, local copies, waits for them, and re-layouts, blend_block(): block_params = splats[:, jnp.maximum(block_lists, 0)]  193 us
    dot_general x16, matrix products, blend_block(): jnp.einsum('tpk,ctk->ctp', weight, block_params[6:9], precision=lax.Preci...  123 us
    dot_general x16, matrix products, blend_block(): jnp.einsum('tpk,kj->tpj', log_keep, strict, precision=lax.Precision.HIGHEST)  121 us
    reduce_sum x16, other arithmetic, blend_block(): return (log_left + jnp.sum(log_keep, axis=2), colour)  77.7 us
    slice x16, local copies, waits for them, and re-layouts, splat_alpha(): params[5][:, None, :] * jnp.exp(power)  29 us
    all_to_all x1, waiting for transfers between devices, on_device(): lax.all_to_all(outgoing, ('gs', 'img'), split_axis=1, concat_axis=1, tile...  20.9 us
  transfers between devices with their start and end apart: 5, of which 4 were waited for; matrix products, arithmetic and copies ran while one was open for 1% of the time, Pallas kernels for 0%

commit v1 on v0

v1 whole, which is shorter than its diff:
```python
import functools

import jax
import jax.numpy as jnp
import numpy as np
from jax import lax
from jax.experimental import pallas as pl
from jax.experimental.pallas import tpu as pltpu
from jax.sharding import PartitionSpec as P

TILE = 16
LANES = 128
SUBS = 8
PARAMS = 9
LOG2E = 1.4426950408889634

coef_zero = 0.28209479177387814
coef_one = 0.4886025119029199
coef_two = [
    1.0925484305920792,
    -1.0925484305920792,
    0.31539156525252005,
    -1.0925484305920792,
    0.5462742152960396,
]
coef_three = [
    -0.5900435899266435,
    2.890611442640554,
    -0.4570457994644658,
    0.3731763325901154,
    -0.4570457994644658,
    1.445305721320277,
    -0.5900435899266435,
]
camera_z = -3000.0
ssim_share = 0.2
stable_one = 0.0001
stable_two = 0.0009


def extended(value, sides, width):
    for axis, dim in sides:
        size, length = (lax.axis_size(axis), value.shape[dim])
        up = [(i, (i + 1) % size) for i in range(size - 1)]
        down = [(j, i) for i, j in up]
        last = lax.slice_in_dim(value, length - width, length, axis=dim)
        first = lax.slice_in_dim(value, 0, width, axis=dim)
        before = lax.ppermute(last, axis, up)
        after = lax.ppermute(first, axis, down)
        value = jnp.concatenate([before, value, after], axis=dim)
    return value


def window():
    offsets = jnp.arange(11, dtype=jnp.float32) - 5.0
    weights = jnp.exp(-offsets * offsets / 4.5)
    return weights / jnp.sum(weights)


def band_matrix(outputs, inputs_len, sign):
    difference = sign * (
        jnp.arange(inputs_len, dtype=jnp.int32)[None, :]
        - jnp.arange(outputs, dtype=jnp.int32)[:, None]
    )
    offsets = jnp.arange(11, dtype=jnp.int32)
    return jnp.sum(
        jnp.where(difference[:, :, None] == offsets[None, None, :], window()[None, None, :], 0.0),
        axis=2,
    )


def loss_from(filtered, rendered, truth):
    mean_r, mean_t = (filtered[0:3], filtered[3:6])
    variance_r = filtered[6:9] - mean_r * mean_r
    variance_t = filtered[9:12] - mean_t * mean_t
    covariance = filtered[12:15] - mean_r * mean_t
    similarity = (
        (2.0 * mean_r * mean_t + stable_one)
        * (2.0 * covariance + stable_two)
        / (
            (mean_r * mean_r + mean_t * mean_t + stable_one)
            * (variance_r + variance_t + stable_two)
        )
    )
    return (1.0 - ssim_share) * jnp.mean(jnp.abs(rendered - truth), axis=0) + ssim_share * (
        1.0 - jnp.mean(similarity, axis=0)
    )


def iota(shape, dim):
    return lax.broadcasted_iota(jnp.int32, shape, dim)


def lane_take(values, index):
    return jnp.take_along_axis(values, index, axis=1, mode="promise_in_bounds")


def sublane_take(values, index):
    return jnp.take_along_axis(values, index, axis=0, mode="promise_in_bounds")


def as_bf16(value):
    return value.astype(jnp.bfloat16).astype(jnp.float32)


def three_parts(value):
    high = as_bf16(value)
    rest = value - high
    middle = as_bf16(rest)
    return high, middle, rest - middle


def project(row):
    mean_x, mean_y, mean_z = row(0), row(1), row(2)
    squared = [jnp.exp(2.0 * row(3 + k)) for k in range(3)]
    quat = [row(6 + k) for k in range(4)]
    norm = jnp.sqrt(quat[0] * quat[0] + quat[1] * quat[1] + quat[2] * quat[2] + quat[3] * quat[3])
    quat_w, quat_x, quat_y, quat_z = [part / norm for part in quat]
    first = [
        1.0 - 2.0 * (quat_y * quat_y + quat_z * quat_z),
        2.0 * (quat_x * quat_y - quat_w * quat_z),
        2.0 * (quat_x * quat_z + quat_w * quat_y),
    ]
    second = [
        2.0 * (quat_x * quat_y + quat_w * quat_z),
        1.0 - 2.0 * (quat_x * quat_x + quat_z * quat_z),
        2.0 * (quat_y * quat_z - quat_w * quat_x),
    ]

    def weighted(left, right):
        return (
            left[0] * right[0] * squared[0]
            + left[1] * right[1] * squared[1]
            + left[2] * right[2] * squared[2]
        )

    cov_xx = weighted(first, first) + 0.3
    cov_xy = weighted(first, second)
    cov_yy = weighted(second, second) + 0.3
    determinant = cov_xx * cov_yy - cov_xy * cov_xy
    log_opacity = -LOG2E * jnp.log(1.0 + jnp.exp(-row(10)))
    delta_z = mean_z - camera_z
    length = jnp.sqrt(mean_x * mean_x + mean_y * mean_y + delta_z * delta_z)
    dir_x, dir_y, dir_z = (mean_x / length, mean_y / length, delta_z / length)
    sq_x, sq_y, sq_z = (dir_x * dir_x, dir_y * dir_y, dir_z * dir_z)
    prod_xy, prod_yz, prod_xz = (dir_x * dir_y, dir_y * dir_z, dir_x * dir_z)
    basis = [
        coef_zero * jnp.ones_like(dir_x),
        -coef_one * dir_y,
        coef_one * dir_z,
        -coef_one * dir_x,
        coef_two[0] * prod_xy,
        coef_two[1] * prod_yz,
        coef_two[2] * (2.0 * sq_z - sq_x - sq_y),
        coef_two[3] * prod_xz,
        coef_two[4] * (sq_x - sq_y),
        coef_three[0] * dir_y * (3.0 * sq_x - sq_y),
        coef_three[1] * prod_xy * dir_z,
        coef_three[2] * dir_y * (4.0 * sq_z - sq_x - sq_y),
        coef_three[3] * dir_z * (2.0 * sq_z - 3.0 * sq_x - 3.0 * sq_y),
        coef_three[4] * dir_x * (4.0 * sq_z - sq_x - sq_y),
        coef_three[5] * dir_z * (sq_x - sq_y),
        coef_three[6] * dir_x * (sq_x - 3.0 * sq_y),
    ]
    colours = []
    for channel in range(3):
        total = row(11 + 16 * channel) * basis[0]
        for k in range(1, 16):
            total = total + row(11 + 16 * channel + k) * basis[k]
        colours.append(jnp.maximum(total + 0.5, 0.0))
    return [
        mean_x,
        mean_y,
        (-0.5 * LOG2E) * (cov_yy / determinant),
        LOG2E * (cov_xy / determinant),
        (-0.5 * LOG2E) * (cov_xx / determinant),
        log_opacity,
    ] + colours


def pack_kernel(cap, gauss_ref, send_ref, out_ref, table_ref, index_ref):
    targets = out_ref.shape[0]
    chunks = gauss_ref.shape[1] // LANES
    spare = LANES - cap
    rows = project(lambda k: gauss_ref[k : k + 1, :])
    for k in range(PARAMS):
        table_ref[k : k + 1, :] = rows[k]
    lane = iota((SUBS, LANES), 1)
    sub = iota((SUBS, LANES), 0)
    send_chunks = send_ref.shape[1] // LANES
    for target in range(targets):
        chunk, shift = divmod(target * cap, LANES)

        def piece(c):
            c = min(c, send_chunks - 1)
            return jnp.broadcast_to(send_ref[0:1, c * LANES : (c + 1) * LANES], (SUBS, LANES))

        index = piece(chunk)
        if shift:
            index = jnp.where(
                lane < LANES - shift,
                pltpu.roll(index, LANES - shift, axis=1),
                pltpu.roll(piece(chunk + 1), LANES - shift, axis=1),
            )
        result = index
        for r in range(-(-cap // spare)):
            moved = pltpu.roll(index, (cap - r * spare) % LANES, axis=1)
            result = jnp.where((lane >= cap) & (sub == r), moved, result)
        index_ref[target] = result

    def one(target, carry):
        index = index_ref[target]
        low, high = index & (LANES - 1), index >> 7
        left = jnp.zeros((SUBS, LANES), jnp.float32)
        right = left
        for c in range(chunks):
            hit = high == c
            part = lane_take(table_ref[0:SUBS, c * LANES : (c + 1) * LANES], low)
            left = jnp.where(hit, part, left)
            last = jnp.broadcast_to(
                table_ref[SUBS : SUBS + 1, c * LANES : (c + 1) * LANES], (SUBS, LANES)
            )
            right = jnp.where(hit, lane_take(last, low), right)
        out_ref[target] = jnp.where(lane < cap, left, right)
        return carry

    lax.fori_loop(0, targets, one, 0)


def sort_kernel(cols_here, lists_ref, index_ref, meta_ref, centre_ref):
    tiles, length = lists_ref.shape
    lists = lists_ref[...]
    live = jnp.sum((lists >= 0).astype(jnp.float32), axis=1, keepdims=True)
    live = jnp.broadcast_to(live, (tiles, tiles))
    down, across = iota((tiles, tiles), 0), iota((tiles, tiles), 1)
    live_row = jnp.sum(jnp.where(down == across, live, 0.0), axis=0, keepdims=True)
    ahead = (live > live_row) | ((live == live_row) & (down < across))
    rank_row = jnp.sum(ahead.astype(jnp.float32), axis=0, keepdims=True)
    behind = (live_row > live) | ((live_row == live) & (across < down))
    rank = jnp.sum(behind.astype(jnp.float32), axis=1, keepdims=True)
    select = (rank_row == down.astype(jnp.float32)).astype(jnp.float32)
    placed = (rank == across.astype(jnp.float32)).astype(jnp.float32)
    live_sorted = jnp.sum(placed * live, axis=0, keepdims=True)
    tile_sorted = jnp.sum(placed * down.astype(jnp.float32), axis=0, keepdims=True)
    meta_ref[0:1, :] = live_sorted.astype(jnp.int32)
    meta_ref[1:2, :] = tile_sorted.astype(jnp.int32)
    tile = jnp.sum(select * across.astype(jnp.float32), axis=1, keepdims=True).astype(jnp.int32)
    tile = jnp.broadcast_to(tile, (tiles, tiles))
    tile_row = lax.div(tile, cols_here)
    tile_col = tile - tile_row * cols_here
    tile_row = tile_row + lax.axis_index("img") * (tiles // cols_here)
    tile_col = tile_col + lax.axis_index("gs") * cols_here
    centre_ref[0] = (tile_col * TILE + TILE // 2).astype(jnp.float32)
    centre_ref[1] = (tile_row * TILE + TILE // 2).astype(jnp.float32)
    high = (lists >> 7).astype(jnp.float32).astype(jnp.bfloat16)
    low = (lists & (LANES - 1)).astype(jnp.float32).astype(jnp.bfloat16)
    select = select.astype(jnp.bfloat16)
    high = jnp.dot(select, high, preferred_element_type=jnp.float32)
    low = jnp.dot(select, low, preferred_element_type=jnp.float32)
    index_ref[...] = high.astype(jnp.int32) * LANES + low.astype(jnp.int32)


def basis_matrix():
    local = np.arange(TILE) - 7.5
    kinds = [[(0, local**0), (1, local), (2, local**2)], [(3, local**0), (4, local)]]
    kinds += [[(k, local**0)] for k in range(5, 9)]
    matrix = np.zeros((2 * LANES, len(kinds) * LANES), np.float32)
    for kind, terms in enumerate(kinds):
        for coefficient, values in terms:
            for part in range(3):
                for t in range(SUBS):
                    start = kind * LANES + t * TILE
                    matrix[(coefficient * 3 + part) * SUBS + t, start : start + TILE] = values
    return jnp.asarray(matrix, jnp.bfloat16)


def render_kernel(
    cap, cols_here, meta_ref, recv_ref, index_ref, centre_ref, basis_ref, out_ref, table_ref, rows_ref
):
    sources = recv_ref.shape[0]
    tiles, list_len = index_ref.shape
    chunks = table_ref.shape[1] // LANES
    spare = LANES - cap
    lane = iota((SUBS, LANES), 1)
    sub = iota((SUBS, LANES), 0)
    for source in range(sources):
        value = recv_ref[source]
        last = jnp.zeros((SUBS, LANES), jnp.float32)
        for r in range(-(-cap // spare)):
            row = jnp.broadcast_to(value[r : r + 1, :], (SUBS, LANES))
            moved = pltpu.roll(row, (r * spare - cap) % LANES, axis=1)
            last = jnp.where((lane >= r * spare) & (lane < (r + 1) * spare), moved, last)
        chunk, shift = divmod(source * cap, LANES)
        here = min(cap, LANES - shift)
        if shift:
            value = pltpu.roll(value, shift, axis=1)
            last = pltpu.roll(last, shift, axis=1)
        for c, start, end, lo in ((chunk, shift, shift + here, 0), (chunk + 1, 0, cap - here, 1)):
            if end > start:
                table_ref[0:SUBS, c * LANES + start : c * LANES + end] = value[:, start:end]
                table_ref[SUBS : SUBS + 1, c * LANES + start : c * LANES + end] = last[0:1, start:end]

    up = (sub.astype(jnp.float32) + 0.5)
    up_squared = up * up
    flip = (SUBS - 1) - sub
    zero = jnp.zeros((SUBS, LANES), jnp.float32)

    def group(g, carry):
        start = pl.multiple_of(g * SUBS, SUBS)
        count = meta_ref[0, g * SUBS]
        centre_x = centre_ref[0, pl.ds(start, SUBS), :]
        centre_y = centre_ref[1, pl.ds(start, SUBS), :]

        def block(b, state):
            index = index_ref[pl.ds(start, SUBS), pl.ds(pl.multiple_of(b * LANES, LANES), LANES)]
            live = index >= 0
            safe = jnp.maximum(index, 0)
            low, high = safe & (LANES - 1), safe >> 7

            def chunk(c, params):
                hit = high == c
                at = pl.ds(pl.multiple_of(c * LANES, LANES), LANES)
                return tuple(
                    jnp.where(
                        hit,
                        lane_take(jnp.broadcast_to(table_ref[p : p + 1, at], (SUBS, LANES)), low),
                        params[p],
                    )
                    for p in range(PARAMS)
                )

            params = lax.fori_loop(0, chunks, chunk, (zero,) * PARAMS, unroll=4)
            u = params[0] - centre_x
            v = params[1] - centre_y
            quad_x, quad_xy, quad_y = params[2:5]
            slope_x = quad_x * u
            slope_y = quad_y * v
            constant = params[5] + slope_x * u + slope_y * v + quad_xy * u * v
            coefficients = [
                jnp.where(live, constant, -1e5),
                jnp.where(live, -2.0 * slope_x - quad_xy * v, 0.0),
                jnp.where(live, quad_x, 0.0),
                jnp.where(live, -2.0 * slope_y - quad_xy * u, 0.0),
                jnp.where(live, quad_xy, 0.0),
                jnp.where(live, quad_y, 0.0),
            ] + list(params[6:9])
            parts = [part for value in coefficients for part in three_parts(value)]
            parts += [zero] * (2 * LANES // SUBS - len(parts))
            stacked = jnp.concatenate(parts, axis=0).T.astype(jnp.bfloat16)
            for kind in range(6):
                rows_ref[kind, 0:LANES, :] = jnp.dot(
                    stacked,
                    basis_ref[:, kind * LANES : (kind + 1) * LANES],
                    preferred_element_type=jnp.float32,
                )
            steps = (jnp.minimum(count - b * LANES, LANES) + SUBS - 1) >> 3

            def eight(s, state):
                left_a, left_b, ra, ga, ba, rb, gb, bb = state
                for q in range(SUBS):
                    def row(kind):
                        return rows_ref[kind, pl.ds(s * SUBS + q, SUBS, stride=0), :]

                    even = row(0) + up_squared * row(2)
                    odd = up * row(1)
                    alpha_a = jnp.exp2(even - odd)
                    alpha_b = jnp.exp2(even + odd)
                    weight_a = left_a * alpha_a
                    weight_b = left_b * alpha_b
                    left_a = left_a - weight_a
                    left_b = left_b - weight_b
                    red, green, blue = row(3), row(4), row(5)
                    ra, ga, ba = ra + weight_a * red, ga + weight_a * green, ba + weight_a * blue
                    rb, gb, bb = rb + weight_b * red, gb + weight_b * green, bb + weight_b * blue
                return left_a, left_b, ra, ga, ba, rb, gb, bb

            return lax.fori_loop(0, steps, eight, state)

        one = jnp.ones((SUBS, LANES), jnp.float32)
        state = lax.fori_loop(
            0, (count + LANES - 1) >> 7, block, (one, one) + (zero,) * 6
        )
        halves = [sublane_take(value, flip) for value in state[2:5]] + list(state[5:8])
        for t in range(SUBS):
            tile = meta_ref[1, g * SUBS + t]
            tile_row = tile // cols_here
            column = (tile - tile_row * cols_here) * TILE
            shift = column & (LANES - 1)
            at = pl.ds(pl.multiple_of(column - shift, LANES), LANES)
            mask = (lane >= shift) & (lane < shift + TILE)
            for half in range(2):
                to = pl.ds(pl.multiple_of(tile_row * TILE + half * SUBS, SUBS), SUBS)
                for channel in range(3):
                    moved = pltpu.roll(
                        halves[half * 3 + channel], (shift - t * TILE) & (LANES - 1), axis=1
                    )
                    pltpu.store(out_ref.at[channel, to, at], moved, mask=mask)
        return carry

    lax.fori_loop(0, tiles // SUBS, group, 0)


VMEM = pl.BlockSpec(memory_space=pltpu.VMEM)
SMEM = pl.BlockSpec(memory_space=pltpu.SMEM)


def on_device(gaussians, send_slots, tile_lists, truth):
    axes = ("gs", "img")
    devices = lax.axis_size(axes)
    cap = send_slots.shape[1] // devices
    count = gaussians.shape[1]
    rows_here, cols_here, list_len = tile_lists.shape
    tiles = rows_here * cols_here
    slots = send_slots.shape[1]
    packed = pl.pallas_call(
        functools.partial(pack_kernel, cap),
        out_shape=jax.ShapeDtypeStruct((devices, SUBS, LANES), jnp.float32),
        in_specs=[VMEM, VMEM],
        out_specs=VMEM,
        scratch_shapes=[
            pltpu.VMEM((2 * SUBS, count), jnp.float32),
            pltpu.VMEM((devices, SUBS, LANES), jnp.int32),
        ],
        name="pack",
    )(gaussians, send_slots)
    arrived = lax.all_to_all(packed, axes, split_axis=0, concat_axis=0, tiled=True)
    index, meta, centre = pl.pallas_call(
        functools.partial(sort_kernel, cols_here),
        out_shape=(
            jax.ShapeDtypeStruct((tiles, list_len), jnp.int32),
            jax.ShapeDtypeStruct((SUBS, tiles), jnp.int32),
            jax.ShapeDtypeStruct((2, tiles, LANES), jnp.float32),
        ),
        in_specs=[VMEM],
        out_specs=(VMEM, VMEM, VMEM),
        name="order",
    )(tile_lists.reshape(tiles, list_len))
    height, width = rows_here * TILE, cols_here * TILE
    rendered = pl.pallas_call(
        functools.partial(render_kernel, cap, cols_here),
        out_shape=jax.ShapeDtypeStruct((3, height, width), jnp.float32),
        in_specs=[SMEM, VMEM, VMEM, VMEM, VMEM],
        out_specs=VMEM,
        scratch_shapes=[
            pltpu.VMEM((2 * SUBS, -(-slots // LANES) * LANES), jnp.float32),
            pltpu.VMEM((6, LANES + SUBS, LANES), jnp.float32),
        ],
        name="render",
    )(meta, arrived, index, centre, basis_matrix())
    stacked = jnp.concatenate([rendered, truth])
    padded = extended(stacked, (("gs", 2), ("img", 1)), 5)
    rim_r, rim_t = (padded[0:3], padded[3:6])
    quantities = jnp.concatenate([rim_r, rim_t, rim_r * rim_r, rim_t * rim_t, rim_r * rim_t])
    band_rows = band_matrix(height, height + 10, 1)
    band_cols = band_matrix(width, width + 10, 1).T
    filtered = jnp.einsum("ij,cjw->ciw", band_rows, quantities, precision=lax.Precision.HIGHEST)
    filtered = jnp.einsum("ciw,wv->civ", filtered, band_cols, precision=lax.Precision.HIGHEST)
    return (rendered, loss_from(filtered, rendered, truth))


def solution(mesh):
    return jax.shard_map(
        on_device,
        mesh=mesh,
        in_specs=(
            P(None, ("gs", "img")),
            P(("gs", "img"), None),
            P("img", "gs", None),
            P(None, "img", "gs"),
        ),
        out_specs=(P(None, "img", "gs"), P("img", "gs")),
        check_vma=False,
    )
```

time: 683 us -> 104 us (0.15)
  the two profiles are of different devices: /device:TPU:0 before, /device:TPU:25 now
where the time goes in v1:
time: 104 us; the launch traced here: 103 us
  Pallas kernels  44.1 us (42%)
  starting transfers between devices  20.8 us (20%)
  waiting for transfers between devices  17.9 us (17%)
  matrix products  13.4 us (13%)
  other arithmetic  5.65 us (5%)
    pallas_call x1, Pallas kernels, on_device(): pl.pallas_call(functools.partial(render_kernel, cap, cols_here), out_shap...  37.1 us
    ppermute x2, waiting for transfers between devices, extended(): after = lax.ppermute(first, axis, down)  12 us
    ppermute x2, starting transfers between devices, extended(): before = lax.ppermute(last, axis, up)  9.06 us
    dot_general x1, matrix products, on_device(): jnp.einsum('ij,cjw->ciw', band_rows, quantities, precision=lax.Precision....  8.59 us
    all_to_all x1, starting transfers between devices, on_device(): lax.all_to_all(packed, axes, split_axis=0, concat_axis=0, tiled=True)  6.16 us
    ppermute x2, starting transfers between devices, extended(): after = lax.ppermute(first, axis, down)  5.56 us
    pallas_call x1, Pallas kernels, on_device(): pl.pallas_call(functools.partial(pack_kernel, cap), out_shape=jax.ShapeDt...  5.07 us
    dot_general x1, matrix products, on_device(): jnp.einsum('ciw,wv->civ', filtered, band_cols, precision=lax.Precision.HI...  4.8 us
  transfers between devices with their start and end apart: 5, of which 4 were waited for; matrix products, arithmetic and copies ran while one was open for 2% of the time, Pallas kernels for 2%

profile of v1, /device:TPU:25, one launch (start us, length us, event | category | flops | bytes accessed | tf_op | source)
XLA Modules:
  0.0 103.3 jit_solution(283981615378485297)
XLA Ops:
  0.6 0.0 copy-start.1
  0.6 5.1 %pack.1 = f32[32,8,128]{2,1,0:T(8,128)} custom-call(f32[59,1280]{1,0:T(8,128)} %gauss_ref.1, s32[1,2560]{1,0:T(1,128)} %send_ref.1), custom_call_target="tpu_custom_call" | custom-call | tf_op jit(solution)/shard_map/pack/pallas_call | solution.py:415
  5.7 6.2 %all-to-all-start = ((f32[32,8,128]{2,1,0:T(8,128)}), f32[32,8,128]{2,1,0:T(8,128)S(1)}, u32[]{:S(2)}, u32[]{:S(2)}) async-start(f32[32,8,128]{2,1,0:T(8,128)} %pack.1), calls=%async_computation | async-start | bytes 262144 | tf_op jit(solution)/shard_map/all_to_all | solution.py:426
  11.9 0.7 fusion.33
  12.6 2.0 %order.1 = (s32[128,512]{1,0:T(8,128)}, s32[8,128]{1,0:T(8,128)}, f32[2,128,128]{2,1,0:T(8,128)}) custom-call(s32[128,512]{1,0:T(8,128)} %bitcast.10), custom_call_target="tpu_custom_call" | custom-call | tf_op jit(solution)/shard_map/order/pallas_call | solution.py:427
  14.6 0.6 broadcast_divide_fusion
  15.2 0.4 select_reduce_fusion
  15.6 1.5 %all-to-all-done.recv_ref = f32[32,8,128]{2,1,0:T(8,128)S(1)} async-done(((f32[32,8,128]{2,1,0:T(8,128)}), f32[32,8,128]{2,1,0:T(8,128)S(1)}, u32[]{:S(2)}, u32[]{:S(2)}) %all-to-all-start) | async-done | bytes 131104 | tf_op jit(solution)/shard_map/all_to_all | solution.py:426
  17.1 0.0 copy-start.2
  17.1 0.7 copy-done.2
  17.8 37.1 %render.1 = f32[3,128,256]{2,1,0:T(8,128)} custom-call(s32[8,128]{1,0:T(8,128)} %get-tuple-element.5.meta_ref, f32[32,8,128]{2,1,0:T(8,128)} %copy-done.2, s32[128,512]{1,0:T(8,128)} %get-tuple-element.6.index_ref, f32[2,128,128]{2,1,0:T(8,128)} %get-tuple-element.7.centre_ref, bf16[256,768]{1,0:T(8,128)(2,1)} %constant.27.clone.basis_ref), custom_call_target="tpu_custom_call" | custom-call | tf_op jit(solution)/shard_map/render/pallas_call | solution.py:439
  54.9 0.0 copy-done.1
  54.9 0.0 copy-start
  54.9 1.2 %fusion.20 = (f32[6,128,5]{2,1,0:T(8,128)S(1)}, f32[6,128,5]{2,1,0:T(8,128)S(1)}) fusion(f32[3,128,256]{2,1,0:T(8,128)} %render.1, f32[3,128,256]{2,1,0:T(8,128)S(1)} %copy-done.1), kind=kLoop, calls=%fused_computation.30 | loop fusion | flops 7680 | bytes 817152 | tf_op jit(solution)/shard_map/concatenate | solution.py:450
  56.1 2.7 %collective-permute-start = (f32[6,128,5]{2,1,0:T(8,128)S(1)}, f32[6,128,5]{2,1,0:T(8,128)S(1)}, u32[]{:S(2)}, u32[]{:S(2)}) collective-permute-start(f32[6,128,5]{2,1,0:T(8,128)S(1)} %get-tuple-element.13), channel_id=1, source_target_pairs={{0,4},{4,8},{8,12},{12,16},{16,20},{20,24},{24,28},{1,5},{5,9},{9,... | collective-permute-start | bytes 46088 | tf_op jit(solution)/shard_map/ppermute | solution.py:48
  58.8 3.5 %collective-permute-start.1 = (f32[6,128,5]{2,1,0:T(8,128)S(1)}, f32[6,128,5]{2,1,0:T(8,128)S(1)}, u32[]{:S(2)}, u32[]{:S(2)}) collective-permute-start(f32[6,128,5]{2,1,0:T(8,128)S(1)} %get-tuple-element.14), channel_id=1, source_target_pairs={{4,0},{8,4},{12,8},{16,12},{20,16},{24,20},{28,24},{5,1},{9,5},{13... | collective-permute-start | bytes 46088 | tf_op jit(solution)/shard_map/ppermute | solution.py:49
  62.3 0.1 select_reduce_fusion.1
  62.4 4.4 %collective-permute-done = f32[6,128,5]{2,1,0:T(8,128)S(1)} collective-permute-done((f32[6,128,5]{2,1,0:T(8,128)S(1)}, f32[6,128,5]{2,1,0:T(8,128)S(1)}, u32[]{:S(2)}, u32[]{:S(2)}) %collective-permute-start) | collective-permute-done | bytes 15392 | tf_op jit(solution)/shard_map/ppermute | solution.py:48
  66.8 8.5 %collective-permute-done.1 = f32[6,128,5]{2,1,0:T(8,128)S(1)} collective-permute-done((f32[6,128,5]{2,1,0:T(8,128)S(1)}, f32[6,128,5]{2,1,0:T(8,128)S(1)}, u32[]{:S(2)}, u32[]{:S(2)}) %collective-permute-start.1) | collective-permute-done | bytes 15392 | tf_op jit(solution)/shard_map/ppermute | solution.py:49
  75.3 0.9 pad_maximum_fusion.5
  76.2 6.3 %collective-permute-start.2 = (f32[6,5,266]{2,1,0:T(8,128)S(1)}, f32[6,5,266]{2,1,0:T(8,128)S(1)}, u32[]{:S(2)}, u32[]{:S(2)}) collective-permute-start(f32[6,5,266]{2,1,0:T(8,128)S(1)} %get-tuple-element.8), channel_id=1, source_target_pairs={{0,1},{1,2},{2,3},{4,5},{5,6},{6,7},{8,9},{9,10},{10,11},{12,13},{... | collective-permute-start | bytes 95768 | tf_op jit(solution)/shard_map/ppermute | solution.py:48
  82.6 2.1 %collective-permute-start.3 = (f32[6,5,266]{2,1,0:T(8,128)S(1)}, f32[6,5,266]{2,1,0:T(8,128)S(1)}, u32[]{:S(2)}, u32[]{:S(2)}) collective-permute-start(f32[6,5,266]{2,1,0:T(8,128)S(1)} %get-tuple-element.9), channel_id=1, source_target_pairs={{1,0},{2,1},{3,2},{5,4},{6,5},{7,6},{9,8},{10,9},{11,10},{13,12},{... | collective-permute-start | bytes 95768 | tf_op jit(solution)/shard_map/ppermute | solution.py:49
  84.7 0.0 copy-done
  84.7 0.1 abs_reduce_fusion
  84.7 0.0 collective-permute-done.2
  84.7 3.5 %collective-permute-done.3 = f32[6,5,266]{2,1,0:T(8,128)S(1)} collective-permute-done((f32[6,5,266]{2,1,0:T(8,128)S(1)}, f32[6,5,266]{2,1,0:T(8,128)S(1)}, u32[]{:S(2)}, u32[]{:S(2)}) %collective-permute-start.3) | collective-permute-done | bytes 31952 | tf_op jit(solution)/shard_map/ppermute | solution.py:49
  88.2 0.5 pad_maximum_fusion
  88.8 0.1 slice_multiply_fusion.2
  88.9 8.6 %fusion = f32[15,266,128]{2,1,0:T(8,128)S(1)} fusion(f32[3,138,266]{2,1,0:T(8,128)S(1)} %get-tuple-element.11, f32[3,138,266]{2,1,0:T(8,128)S(1)} %get-tuple-element.12, f32[3,138,266]{2,1,0:T(8,128)S(1)} %get-tuple-element.10, f32[6,5,266]{2,1,0:T(8,128)S(1)} %collective-permute-done.3, f32[6,128,5]{2,1,0:T(8,128)S(1)} %collective-permute-done.1, ...), kind=kOutput, calls=%fused_computation | convolution fusion | flops 850157312 | bytes 4316016 | tf_op jit(solution)/shard_map/ij,cjw->ciw/dot_general | solution.py:456
  97.5 4.8 %fusion.18 = f32[15,128,256]{2,1,0:T(8,128)S(1)} fusion(f32[15,266,128]{2,1,0:T(8,128)S(1)} %fusion, f32[256,266]{0,1:T(8,128)S(1)} %select_reduce_fusion), kind=kOutput, calls=%fused_computation.20 | convolution fusion | flops 1568931840 | bytes 4281344 | tf_op jit(solution)/shard_map/ciw,wv->civ/dot_general | solution.py:457
  102.3 0.3 fusion.28
  102.6 0.7 multiply_add_fusion
  (2 shorter events, 0.0 us)
Async XLA Ops:
  0.6 54.2 %copy-start.1 = (f32[3,128,256]{2,1,0:T(8,128)S(1)}, f32[3,128,256]{2,1,0:T(8,128)}, u32[]{:S(2)}) copy-start(f32[3,128,256]{2,1,0:T(8,128)} %param.8) | copy-start | bytes 1179652
  5.7 11.4 %all-to-all-start = ((f32[32,8,128]{2,1,0:T(8,128)}), f32[32,8,128]{2,1,0:T(8,128)S(1)}, u32[]{:S(2)}, u32[]{:S(2)}) async-start(f32[32,8,128]{2,1,0:T(8,128)} %pack.1), calls=%async_computation | async-start | bytes 262144 | tf_op jit(solution)/shard_map/all_to_all | solution.py:426
  17.1 0.7 copy-start.2
  54.9 29.8 %copy-start = (f32[3,128,256]{2,1,0:T(8,128)S(1)}, f32[3,128,256]{2,1,0:T(8,128)}, u32[]{:S(2)}) copy-start(f32[3,128,256]{2,1,0:T(8,128)} %render.1) | copy-start | bytes 1179652
  56.1 10.7 %collective-permute-start = (f32[6,128,5]{2,1,0:T(8,128)S(1)}, f32[6,128,5]{2,1,0:T(8,128)S(1)}, u32[]{:S(2)}, u32[]{:S(2)}) collective-permute-start(f32[6,128,5]{2,1,0:T(8,128)S(1)} %get-tuple-element.13), channel_id=1, source_target_pairs={{0,4},{4,8},{8,12},{12,16},{16,20},{20,24},{24,28},{1,5},{5,9},{9,... | collective-permute-start | bytes 46088 | tf_op jit(solution)/shard_map/ppermute | solution.py:48
  58.8 16.5 %collective-permute-start.1 = (f32[6,128,5]{2,1,0:T(8,128)S(1)}, f32[6,128,5]{2,1,0:T(8,128)S(1)}, u32[]{:S(2)}, u32[]{:S(2)}) collective-permute-start(f32[6,128,5]{2,1,0:T(8,128)S(1)} %get-tuple-element.14), channel_id=1, source_target_pairs={{4,0},{8,4},{12,8},{16,12},{20,16},{24,20},{28,24},{5,1},{9,5},{13... | collective-permute-start | bytes 46088 | tf_op jit(solution)/shard_map/ppermute | solution.py:49
  76.2 8.5 %collective-permute-start.2 = (f32[6,5,266]{2,1,0:T(8,128)S(1)}, f32[6,5,266]{2,1,0:T(8,128)S(1)}, u32[]{:S(2)}, u32[]{:S(2)}) collective-permute-start(f32[6,5,266]{2,1,0:T(8,128)S(1)} %get-tuple-element.8), channel_id=1, source_target_pairs={{0,1},{1,2},{2,3},{4,5},{5,6},{6,7},{8,9},{9,10},{10,11},{12,13},{... | collective-permute-start | bytes 95768 | tf_op jit(solution)/shard_map/ppermute | solution.py:48
  82.6 5.7 %collective-permute-start.3 = (f32[6,5,266]{2,1,0:T(8,128)S(1)}, f32[6,5,266]{2,1,0:T(8,128)S(1)}, u32[]{:S(2)}, u32[]{:S(2)}) collective-permute-start(f32[6,5,266]{2,1,0:T(8,128)S(1)} %get-tuple-element.9), channel_id=1, source_target_pairs={{1,0},{2,1},{3,2},{5,4},{6,5},{7,6},{9,8},{10,9},{11,10},{13,12},{... | collective-permute-start | bytes 95768 | tf_op jit(solution)/shard_map/ppermute | solution.py:49
